TPU v7x, 32 devices: a whole 2x2x4 slice. The times are simulated.
32 devices in a mesh: req: 8 (over z, x), grp: 4 (over y, core).
Axes of the slice: x: 2, y: 2, z: 4, core: 2. Of those that a mesh axis runs over, the one named last changes fastest.
Arguments:
- hidden: bfloat16 [256, 16, 1024], P(('grp', 'req')), parts along dimension 0, may hold values from -6 to 6
- norm_gain: float32 [1024], replicated, may hold values from 0.1 to 1.9
- in_weight: bfloat16 [1024, 4096], replicated, may hold values from -0.1875 to 0.1875
- conv_weight: float32 [4, 2048], P(None, 'req'), may hold values from -3 to 3
- conv_bias: float32 [2048], P('req'), may hold values from -3 to 3
- x_weight: bfloat16 [2048, 160], P('req'), may hold values from -0.125 to 0.125
- step_weight: bfloat16 [128, 2048], P(None, 'req'), may hold values from -0.5 to 0.5
- step_bias: float32 [2048], P('req'), may hold values from -5 to -1
- log_decay: float32 [16, 2048], P(None, 'req'), may hold values from -0.7 to 2.8
- skip_gain: float32 [2048], P('req'), may hold values from 0.5 to 1.5
- out_weight: bfloat16 [2048, 1024], replicated, may hold values from -0.125 to 0.125
- old_states: float32 [256, 16, 2048], P(('grp', 'req')), parts along dimension 0, may hold values from -3 to 3
- old_edges: bfloat16 [256, 3, 2048], P(('grp', 'req')), parts along dimension 0, may hold values from -6 to 6
- anchor: int32 [256], P('grp'), parts along dimension 0, may hold values from 0 to 63, each once
- fresh_flag: int32 [256], P('grp'), parts along dimension 0, may hold values 0 or 1
- accepted: int32 [256], P('grp'), parts along dimension 0, may hold values from 1 to 16
- request_ages: int32 [256], P('grp'), parts along dimension 0, may hold values from 0 to 7
Outputs:
- layer_out: bfloat16 [256, 16, 1024], P(('grp', 'req')), parts along dimension 0
- new_states: float32 [256, 16, 2048], P(('grp', 'req')), parts along dimension 0
There are 4 independent parts, one for each index of `grp`. A program takes and returns all parts, laid end to end along the dimension named above; an argument that names none is the same for every part. Nothing has to cross between parts.
Inputs may be any that keep to these rules, and one draw needn't show every extreme that they name: Every old slot is the anchor of exactly one request.
All inputs are finite; a program needn't handle non-finite values.
Results may differ from a plain program's by a relative error of at most 0.0091.
Values may be sent and summed in bfloat16 or wider, within the bound.
No kernel may reach another device: no remote copies, remote signals or barrier semaphores. Data moves between devices by JAX's collectives and lax.ppermute only.
A program may use at most 128 MiB of HBM per device.

v0:
```python
import jax
import jax.numpy as jnp
from jax import lax
from jax.sharding import PartitionSpec as P

EPS = 1e-05


def rms_normed(values_in, norm_gain):
    values = values_in.astype(jnp.float32)
    factor = lax.rsqrt(jnp.mean(values * values, axis=-1, keepdims=True) + EPS)
    return (values * factor * norm_gain).astype(jnp.bfloat16)


def on_device(
    hidden,
    norm_gain,
    in_weight,
    conv_weight,
    conv_bias,
    x_weight,
    step_weight,
    step_bias,
    log_decay,
    skip_gain,
    out_weight,
    old_states,
    old_edges,
    anchor,
    fresh_flag,
    accepted,
    request_ages,
):
    local_reqs, draft_len, width = hidden.shape
    inner_width = out_weight.shape[0]
    channels = conv_weight.shape[1]
    state_size = log_decay.shape[0]
    low_rank = step_weight.shape[0]
    span = old_edges.shape[1]
    state_lead = jnp.swapaxes(old_states, 0, 1)
    edge_lead = jnp.swapaxes(old_edges.astype(jnp.float32), 0, 1)
    moved_states, moved_edges = (
        lax.all_to_all(state_lead, "req", split_axis=2, concat_axis=1, tiled=True),
        lax.all_to_all(edge_lead, "req", split_axis=2, concat_axis=1, tiled=True),
    )
    token_major = jnp.swapaxes(hidden, 0, 1).reshape(draft_len * local_reqs, width)
    normed = rms_normed(token_major, norm_gain)
    projected = jnp.dot(normed, in_weight, preferred_element_type=jnp.float32).astype(jnp.bfloat16)
    projected = jnp.moveaxis(projected.reshape(draft_len, local_reqs, 2, inner_width), 2, 0)
    grouped = lax.all_to_all(projected, "req", split_axis=3, concat_axis=2, tiled=True)
    all_reqs = grouped.shape[2]
    inner_part = grouped[0]
    gate_part = grouped[1]
    keep_state = (1 - fresh_flag).astype(jnp.float32)
    start_state = jnp.take(moved_states, anchor, axis=1) * keep_state[None, :, None]
    edges = jnp.take(moved_edges, anchor, axis=1)
    distance = span - jnp.arange(span, dtype=jnp.int32)
    usable = (distance[:, None] <= request_ages[None, :]) & (fresh_flag[None, :] == 0)
    history = jnp.where(usable[:, :, None], edges, jnp.zeros((), jnp.float32))
    sequence = jnp.concatenate([history, inner_part.astype(jnp.float32)], axis=0)
    running = conv_bias + conv_weight[0] * sequence[0:draft_len]
    for offset in range(1, conv_weight.shape[0]):
        running = running + conv_weight[offset] * sequence[offset : offset + draft_len]
    conv_out = jax.nn.silu(running).astype(jnp.bfloat16)
    conv_rows = conv_out.reshape(draft_len * all_reqs, channels)
    partial_value = jnp.dot(conv_rows, x_weight, preferred_element_type=jnp.float32)
    mixed_rows = lax.psum(partial_value, "req").astype(jnp.bfloat16)
    flat = all_reqs * channels
    step_sizes = jax.nn.softplus(
        jnp.dot(mixed_rows[:, :low_rank], step_weight, preferred_element_type=jnp.float32)
        + step_bias
    )
    step_sizes = step_sizes.reshape(draft_len, flat)
    coeffs = (
        mixed_rows[:, low_rank:].astype(jnp.float32).reshape(draft_len, all_reqs, 2 * state_size)
    )
    b_coeff = coeffs[:, :, :state_size]
    c_coeff = coeffs[:, :, state_size:]
    inputs = conv_out.astype(jnp.float32)
    flat_inputs = inputs.reshape(draft_len, flat)
    decay = jnp.broadcast_to(
        (-jnp.exp(log_decay))[:, None, :], (state_size, all_reqs, channels)
    ).reshape(state_size, flat)
    start_flat = start_state.reshape(state_size, flat)

    def spread(per_token):
        return jnp.broadcast_to(
            jnp.swapaxes(per_token, 0, 1)[:, :, None], (state_size, all_reqs, channels)
        ).reshape(state_size, flat)

    def advance(carried, sliced):
        current, chosen = carried
        step_delta, step_b, step_c, step_input, step_index = sliced
        factor = jnp.exp(step_delta[None, :] * decay)
        current = factor * current + (step_delta * step_input)[None, :] * spread(step_b)
        result = jnp.sum(spread(step_c) * current, axis=0)
        picked = jnp.broadcast_to(
            (accepted == step_index + 1)[:, None], (all_reqs, channels)
        ).reshape(flat)
        chosen = jnp.where(picked[None, :], current, chosen)
        return ((current, chosen), result)

    sliced = (step_sizes, b_coeff, c_coeff, flat_inputs, jnp.arange(draft_len, dtype=jnp.int32))
    (final_state, chosen), outputs = lax.scan(advance, (start_flat, start_flat), sliced)
    outputs = outputs.reshape(draft_len, all_reqs, channels)
    gated_rows = (
        (outputs + skip_gain * inputs) * jax.nn.silu(gate_part.astype(jnp.float32))
    ).astype(jnp.bfloat16)
    returned = lax.all_to_all(gated_rows, "req", split_axis=1, concat_axis=2, tiled=True)
    layer_out = jnp.dot(
        returned.reshape(draft_len * local_reqs, inner_width),
        out_weight,
        preferred_element_type=jnp.float32,
    ).astype(jnp.bfloat16)
    layer_out = jnp.swapaxes(layer_out.reshape(draft_len, local_reqs, width), 0, 1)
    owned = lax.all_to_all(
        chosen.reshape(state_size, all_reqs, channels),
        "req",
        split_axis=1,
        concat_axis=2,
        tiled=True,
    )
    return (layer_out, jnp.swapaxes(owned, 0, 1))


def solution(mesh):
    return jax.shard_map(
        on_device,
        mesh=mesh,
        in_specs=(
            P(("grp", "req"), None, None),
            P(),
            P(),
            P(None, "req"),
            P("req"),
            P("req", None),
            P(None, "req"),
            P("req"),
            P(None, "req"),
            P("req"),
            P(),
            P(("grp", "req"), None, None),
            P(("grp", "req"), None, None),
            P("grp"),
            P("grp"),
            P("grp"),
            P("grp"),
        ),
        out_specs=(P(("grp", "req"), None, None), P(("grp", "req"), None, None)),
        check_vma=False,
    )
```

profile of v0, /device:TPU:0, one launch (start us, length us, event | category | flops | bytes accessed | tf_op | source)
XLA Modules:
  0.0 369.8 jit_solution(14479661632174473123)
XLA Ops:
  0.7 4.0 %copy.100 = f32[8,3,2048]{0,1,2:T(4,128)} copy(bf16[8,3,2048]{2,0,1:T(8,128)(2,1)} %param.31) | data formatting | bytes 294912 | tf_op jit(solution)/shard_map/transpose | solution.py:41
  4.7 3.9 %bitcast_bitcast_fusion.2 = f32[2048,3,8]{2,1,0:T(4,128)} fusion(f32[8,3,2048]{0,1,2:T(4,128)} %copy.100), kind=kLoop, calls=%fused_computation.72 | loop fusion | bytes 393216
  8.6 5.1 %reshape.188 = f32[8,1,6144]{2,1,0:T(1,128)} reshape(f32[2048,3,8]{2,1,0:T(4,128)} %bitcast_bitcast_fusion.2) | data formatting | bytes 393216
  13.7 7.3 %all-to-all-start.1 = ((f32[8,1,6144]{2,1,0:T(1,128)}), f32[8,1,6144]{2,1,0:T(1,128)S(1)}, u32[]{:S(2)}, u32[]{:S(2)}) async-start(f32[8,1,6144]{2,1,0:T(1,128)} %reshape.188), calls=%async_computation.1 | async-start | bytes 393216 | tf_op jit(solution)/shard_map/all_to_all | solution.py:44
  20.9 4.7 %copy.94 = f32[8,16,2048]{1,0,2:T(8,128)} copy(f32[8,16,2048]{2,1,0:T(8,128)S(1)} %copy-done.3) | data formatting | bytes 2097152 | tf_op args[11]
  26.0 4.8 %convolution_convert_fusion = bf16[128,4096]{1,0:T(8,128)(2,1)S(1)} fusion(bf16[1024,4096]{1,0:T(8,128)(2,1)} %param.21, f32[1024]{0:T(1024)S(1)} %copy-done.4, f32[128]{0:T(128)S(1)} %rsqrt.12, bf16[8,16,1024]{2,1,0:T(8,128)(2,1)S(1)} %copy-done.2), kind=kOutput, calls=%fused_computation.11 | convolution fusion | flops 1074790400 | bytes 9703936 | tf_op jit(solution)/shard_map/dot_general | solution.py:48
  30.8 8.9 %copy.103 = bf16[16,8,2,2048]{0,1,2,3:T(8,128)(2,1)} copy(bf16[16,8,2,2048]{3,1,2,0:T(8,128)(2,1)S(1)} %bitcast.169) | data formatting | bytes 2097152 | tf_op jit(solution)/shard_map/reshape | solution.py:49
  39.6 7.5 %bitcast_bitcast_fusion = bf16[2048,2,8,16]{3,2,1,0:T(8,128)(2,1)} fusion(bf16[16,8,2,2048]{0,1,2,3:T(8,128)(2,1)} %copy.103), kind=kLoop, calls=%fused_computation.70 | loop fusion | bytes 2097152
  47.1 5.8 %bitcast_bitcast_fusion.1 = f32[2048,8,16]{2,1,0:T(8,128)} fusion(f32[8,16,2048]{1,0,2:T(8,128)} %copy.94), kind=kLoop, calls=%fused_computation.71 | loop fusion | bytes 2097152
  52.9 8.1 %reshape.184 = f32[8,1,32768]{2,1,0:T(1,128)} reshape(f32[2048,8,16]{2,1,0:T(8,128)} %bitcast_bitcast_fusion.1) | data formatting | bytes 2097152
  61.1 6.0 %all-to-all-start = ((f32[8,1,32768]{2,1,0:T(1,128)}), f32[8,1,32768]{2,1,0:T(1,128)S(1)}, u32[]{:S(2)}, u32[]{:S(2)}) async-start(f32[8,1,32768]{2,1,0:T(1,128)} %reshape.184), calls=%async_computation | async-start | bytes 2097152 | tf_op jit(solution)/shard_map/all_to_all | solution.py:43
  67.3 11.3 %reshape.186 = bf16[8,2,32768]{2,1,0:T(2,128)(2,1)} reshape(bf16[2048,2,8,16]{3,2,1,0:T(8,128)(2,1)} %bitcast_bitcast_fusion) | data formatting | bytes 2097152
  80.5 4.7 %reshape.189 = f32[2048,3,8]{2,1,0:T(4,128)} reshape(f32[8,6144]{1,0:T(8,128)S(1)} %reduce.3) | data formatting | bytes 393216
  85.2 3.5 copy.101
  89.6 2.9 all-to-all-done
  92.5 3.7 %all-to-all-start.2 = ((bf16[8,2,32768]{2,1,0:T(2,128)(2,1)}), bf16[8,2,32768]{2,1,0:T(2,128)(2,1)S(1)}, u32[]{:S(2)}, u32[]{:S(2)}) async-start(bf16[8,2,32768]{2,1,0:T(2,128)(2,1)} %reshape.186), calls=%async_computation.2 | async-start | bytes 2097152 | tf_op jit(solution)/shard_map/all_to_all | solution.py:50
  96.3 3.1 reduce.2
  99.4 6.1 %reshape.185 = f32[2048,8,16]{2,1,0:T(8,128)} reshape(f32[8,32768]{1,0:T(8,128)S(1)} %reduce.2) | data formatting | bytes 2097152
  105.5 5.4 %copy.96 = f32[16,8,8,256]{3,2,1,0:T(8,128)S(1)} copy(f32[16,8,8,256]{0,2,3,1:T(8,128)} %bitcast.155) | data formatting | bytes 2097152 | tf_op jit(solution)/shard_map/all_to_all | solution.py:43
  112.4 9.5 %all-to-all-done.2 = bf16[8,2,32768]{2,1,0:T(2,128)(2,1)S(1)} async-done(((bf16[8,2,32768]{2,1,0:T(2,128)(2,1)}), bf16[8,2,32768]{2,1,0:T(2,128)(2,1)S(1)}, u32[]{:S(2)}, u32[]{:S(2)}) %all-to-all-start.2) | async-done | bytes 1048608 | tf_op jit(solution)/shard_map/all_to_all | solution.py:50
  121.9 7.6 %reshape.187 = bf16[2048,2,8,16]{3,2,1,0:T(8,128)(2,1)} reshape(bf16[8,2,32768]{2,1,0:T(2,128)(2,1)S(1)} %all-to-all-done.2) | data formatting | bytes 2097152
  129.5 8.9 %copy.104 = bf16[2,16,8,8,256]{4,2,3,1,0:T(8,128)(2,1)S(1)} copy(bf16[2,16,8,8,256]{1,2,0,4,3:T(8,128)(2,1)} %bitcast.156) | data formatting | bytes 2097152 | tf_op jit(solution)/shard_map/all_to_all | solution.py:50
  140.2 43.6 %all-reduce.1 = bf16[1024,160]{0,1:T(8,128)(2,1)} all-reduce(f32[1024,160]{0,1:T(8,128)S(1)} %fusion.29), channel_id=1, replica_groups=mesh['req'=8,'grp'=4] {'req'}, use_global_device_ids=true, to_apply=%region_1.2 | all-reduce | flops 163840 | bytes 983040 | tf_op jit(solution)/shard_map/psum | solution.py:67
  184.7 2.7 compare_select_fusion
  187.4 2.4 reshape.145
  191.2 132.7 %while.15 = (s32[]{:T(128)}, f32[16,16384]{1,0:T(8,128)S(1)}, f32[16,16384]{1,0:T(8,128)S(1)}, f32[16,16384]{1,0:T(8,128)}, f32[16,16384]{1,0:T(8,128)}, /*index...) while((s32[]{:T(128)}, f32[16,16384]{1,0:T(8,128)S(1)}, ...), condition=%wide.region_4.5_spmd.clone, body=%wide.region_2.4_spmd.clone.sunk | while | flops 1835075 | bytes 18522676 | solution.py:104
  197.6 1.9 dynamic_update_slice.6
  205.9 1.9 dynamic_update_slice.6
  214.2 1.9 dynamic_update_slice.6
  222.5 1.9 dynamic_update_slice.6
  230.7 1.9 dynamic_update_slice.6
  239.0 1.9 dynamic_update_slice.6
  247.3 1.9 dynamic_update_slice.6
  255.6 1.9 dynamic_update_slice.6
  263.9 1.9 dynamic_update_slice.6
  272.2 1.9 dynamic_update_slice.6
  280.5 1.9 dynamic_update_slice.6
  288.8 1.9 dynamic_update_slice.6
  297.1 1.9 dynamic_update_slice.6
  305.4 1.9 dynamic_update_slice.6
  313.7 1.9 dynamic_update_slice.6
  322.0 1.9 dynamic_update_slice.6
  328.1 3.5 all-to-all-start.3
  332.7 9.4 %all-to-all-done.3 = bf16[16,64,256]{2,0,1:T(8,128)(2,1)S(1)} async-done(((bf16[16,64,256]{2,0,1:T(8,128)(2,1)}), bf16[16,64,256]{2,0,1:T(8,128)(2,1)S(1)}, u32[]{:S(2)}, u32[]{:S(2)}) %all-to-all-start.3) | async-done | bytes 524320 | tf_op jit(solution)/shard_map/all_to_all | solution.py:109
  342.1 9.1 %all-to-all-start.4 = ((f32[16,64,256]{2,0,1:T(8,128)}), f32[16,64,256]{2,0,1:T(8,128)S(1)}, u32[]{:S(2)}, u32[]{:S(2)}) async-start(f32[16,64,256]{2,0,1:T(8,128)} %bitcast.121), calls=%async_computation.4 | async-start | bytes 2097152 | tf_op jit(solution)/shard_map/all_to_all | solution.py:116
  351.6 2.9 fusion.2
  355.4 12.2 %all-to-all-done.4 = f32[16,64,256]{2,0,1:T(8,128)S(1)} async-done(((f32[16,64,256]{2,0,1:T(8,128)}), f32[16,64,256]{2,0,1:T(8,128)S(1)}, u32[]{:S(2)}, u32[]{:S(2)}) %all-to-all-start.4) | async-done | bytes 1048608 | tf_op jit(solution)/shard_map/all_to_all | solution.py:116
  368.2 1.6 copy.113
  (299 shorter events, 105.4 us)
Async XLA Ops:
  0.6 139.3 %copy-start = (bf16[256,160]{0,1:T(8,128)(2,1)S(1)}, bf16[256,160]{0,1:T(8,128)(2,1)}, u32[]{:S(2)}) copy-start(bf16[256,160]{0,1:T(8,128)(2,1)} %param.24) | copy-start | bytes 245764
  0.6 20.3 %copy-start.3 = (f32[8,16,2048]{2,1,0:T(8,128)S(1)}, f32[8,16,2048]{2,1,0:T(8,128)}, u32[]{:S(2)}) copy-start(f32[8,16,2048]{2,1,0:T(8,128)} %param.30) | copy-start | bytes 3145732
  8.6 17.1 %copy-start.2 = (bf16[8,16,1024]{2,1,0:T(8,128)(2,1)S(1)}, bf16[8,16,1024]{2,1,0:T(8,128)(2,1)}, u32[]{:S(2)}) copy-start(bf16[8,16,1024]{2,1,0:T(8,128)(2,1)} %param.19) | copy-start | bytes 786436
  8.6 17.4 %copy-start.4 = (f32[1024]{0:T(1024)S(1)}, f32[1024]{0:T(1024)}, u32[]{:S(2)}) copy-start(f32[1024]{0:T(1024)} %param.20) | copy-start | bytes 12292
  13.7 47.4 %all-to-all-start.1 = ((f32[8,1,6144]{2,1,0:T(1,128)}), f32[8,1,6144]{2,1,0:T(1,128)S(1)}, u32[]{:S(2)}, u32[]{:S(2)}) async-start(f32[8,1,6144]{2,1,0:T(1,128)} %reshape.188), calls=%async_computation.1 | async-start | bytes 393216 | tf_op jit(solution)/shard_map/all_to_all | solution.py:44
  52.9 8.2 %copy-start.12 = (s32[64]{0:T(128)S(1)}, s32[64]{0:T(128)}, u32[]{:S(2)}) copy-start(s32[64]{0:T(128)} %param.33) | copy-start | bytes 772
  52.9 14.3 %copy-start.13 = (s32[64]{0:T(128)S(1)}, s32[64]{0:T(128)}, u32[]{:S(2)}) copy-start(s32[64]{0:T(128)} %param.32) | copy-start | bytes 772
  52.9 25.7 %copy-start.9 = (s32[64]{0:T(128)S(1)}, s32[64]{0:T(128)}, u32[]{:S(2)}) copy-start(s32[64]{0:T(128)} %param.35) | copy-start | bytes 772
  52.9 25.9 %copy-start.6 = (f32[4,256]{1,0:T(4,128)S(1)}, f32[4,256]{1,0:T(4,128)}, u32[]{:S(2)}) copy-start(f32[4,256]{1,0:T(4,128)} %param.22) | copy-start | bytes 12292
  52.9 25.9 %copy-start.5 = (f32[16,256]{1,0:T(8,128)S(1)}, f32[16,256]{1,0:T(8,128)}, u32[]{:S(2)}) copy-start(f32[16,256]{1,0:T(8,128)} %param.27) | copy-start | bytes 49156
  61.1 31.4 %all-to-all-start = ((f32[8,1,32768]{2,1,0:T(1,128)}), f32[8,1,32768]{2,1,0:T(1,128)S(1)}, u32[]{:S(2)}, u32[]{:S(2)}) async-start(f32[8,1,32768]{2,1,0:T(1,128)} %reshape.184), calls=%async_computation | async-start | bytes 2097152 | tf_op jit(solution)/shard_map/all_to_all | solution.py:43
  92.5 29.4 %all-to-all-start.2 = ((bf16[8,2,32768]{2,1,0:T(2,128)(2,1)}), bf16[8,2,32768]{2,1,0:T(2,128)(2,1)S(1)}, u32[]{:S(2)}, u32[]{:S(2)}) async-start(bf16[8,2,32768]{2,1,0:T(2,128)(2,1)} %reshape.186), calls=%async_computation.2 | async-start | bytes 2097152 | tf_op jit(solution)/shard_map/all_to_all | solution.py:50
  112.4 27.0 %copy-start.7 = (f32[256]{0:T(256)S(1)}, f32[256]{0:T(256)}, u32[]{:S(2)}) copy-start(f32[256]{0:T(256)} %param.23) | copy-start | bytes 3076
  129.5 55.2 %copy-start.10 = (bf16[128,256]{1,0:T(8,128)(2,1)S(1)}, bf16[128,256]{1,0:T(8,128)(2,1)}, u32[]{:S(2)}) copy-start(bf16[128,256]{1,0:T(8,128)(2,1)} %param.25) | copy-start | bytes 196612
  129.5 55.2 %copy-start.11 = (f32[256]{0:T(256)S(1)}, f32[256]{0:T(256)}, u32[]{:S(2)}) copy-start(f32[256]{0:T(256)} %param.26) | copy-start | bytes 3076
  138.4 1.0 copy-start.1
  138.4 52.8 %copy-start.14 = (s32[64]{0:T(128)S(1)}, s32[64]{0:T(128)}, u32[]{:S(2)}) copy-start(s32[64]{0:T(128)} %param.34) | copy-start | bytes 772
  191.2 134.3 %copy-start.8 = (f32[256]{0:T(256)S(1)}, f32[256]{0:T(256)}, u32[]{:S(2)}) copy-start(f32[256]{0:T(256)} %param.28) | copy-start | bytes 3076
  328.1 14.0 %all-to-all-start.3 = ((bf16[16,64,256]{2,0,1:T(8,128)(2,1)}), bf16[16,64,256]{2,0,1:T(8,128)(2,1)S(1)}, u32[]{:S(2)}, u32[]{:S(2)}) async-start(bf16[16,64,256]{2,0,1:T(8,128)(2,1)} %copy.108), calls=%async_computation.3 | async-start | bytes 1048576 | tf_op jit(solution)/shard_map/all_to_all | solution.py:109
  342.1 25.5 %all-to-all-start.4 = ((f32[16,64,256]{2,0,1:T(8,128)}), f32[16,64,256]{2,0,1:T(8,128)S(1)}, u32[]{:S(2)}, u32[]{:S(2)}) async-start(f32[16,64,256]{2,0,1:T(8,128)} %bitcast.121), calls=%async_computation.4 | async-start | bytes 2097152 | tf_op jit(solution)/shard_map/all_to_all | solution.py:116
where the time goes:
time: 372 us; the launch traced here: 370 us
  local copies, waits for them, and re-layouts  191 us (51%)
  other arithmetic  47.8 us (13%)
  blocking collectives  43.6 us (12%)
  waiting for transfers between devices  33.9 us (9%)
  starting transfers between devices  29.5 us (8%)
  loops' own time  12.3 us (3%)
  matrix products  10.8 us (3%)
    unnamed x47, local copies, waits for them, and re-layouts  70.4 us
    psum x1, blocking collectives, on_device(): mixed_rows = lax.psum(partial_value, 'req').astype(jnp.bfloat16)  43.6 us
    dynamic_update_slice x16, local copies, waits for them, and re-layouts, on_device(): lax.scan(advance, (start_flat, start_flat), sliced)  31.1 us
    while x48, local copies, waits for them, and re-layouts  29.4 us
    dynamic_slice x16, other arithmetic, on_device(): lax.scan(advance, (start_flat, start_flat), sliced)  20.9 us
    reduce_sum x16, other arithmetic, advance(): result = jnp.sum(spread(step_c) * current, axis=0)  14.9 us
    another operation x1, loops' own time, on_device(): lax.scan(advance, (start_flat, start_flat), sliced)  12.3 us
    all_to_all x1, waiting for transfers between devices, on_device(): lax.all_to_all(chosen.reshape(state_size, all_reqs, channels), 'req', spl...  12.2 us
  transfers between devices with their start and end apart: 5, of which 4 were waited for; matrix products, arithmetic and copies ran while one was open for 23% of the time, Pallas kernels for 0%

commit v1 on v0

--- a/solution.py
+++ b/solution.py
@@ -4,6 +4,14 @@
 from jax.sharding import PartitionSpec as P
 
 EPS = 1e-05
+
+
+def _register_trails(view, ndim_at, d0=1):
+    base_arr = lax.psum(1, "req")
+    finding = jnp.split(view, base_arr, ndim_at)
+    later = jnp.stack(finding, axis=0)
+    d_next = lax.all_to_all(later, "req", 0, 0)
+    return jnp.concatenate(d_next, d0)
 
 
 def rms_normed(values_in, norm_gain):
@@ -40,7 +48,7 @@
     state_lead = jnp.swapaxes(old_states, 0, 1)
     edge_lead = jnp.swapaxes(old_edges.astype(jnp.float32), 0, 1)
     moved_states, moved_edges = (
-        lax.all_to_all(state_lead, "req", split_axis=2, concat_axis=1, tiled=True),
+        _register_trails(state_lead, 2),
         lax.all_to_all(edge_lead, "req", split_axis=2, concat_axis=1, tiled=True),
     )
     token_major = jnp.swapaxes(hidden, 0, 1).reshape(draft_len * local_reqs, width)

time: 372 us -> 350 us (0.941)
  local copies, waits for them, and re-layouts: 191 us -> 164 us
  waiting for transfers between devices: 33.9 us -> 47.5 us
    unnamed x47 -> x52, local copies, waits for them, and re-layouts: 70.4 us -> 50.3 us
    all_to_all x1, waiting for transfers between devices: 9.5 us -> 23.9 us  [on_device(): lax.all_to_all(projected, 'req', split_axis=3, concat_axis=2, tiled=True)]
    all_to_all x3 -> x0, local copies, waits for them, and re-layouts: 6.51 us -> none  [on_device(): lax.all_to_all(state_lead, 'req', split_axis=2, concat_axis=1, tiled=True)]
    all_to_all x1, starting transfers between devices: 9.06 us -> 3.78 us  [on_device(): lax.all_to_all(chosen.reshape(state_size, all_reqs, channels), 'req', spl...]
  transfers between devices with their start and end apart: 5 -> 5, of which waited for: 4 -> 3; matrix products, arithmetic and copies ran while one was open for 23% -> 16% of each run, Pallas kernels for 0% -> 0%
where the time goes in v1:
time: 350 us; the launch traced here: 348 us
  local copies, waits for them, and re-layouts  164 us (47%)
  waiting for transfers between devices  47.5 us (14%)
  other arithmetic  44.6 us (13%)
  blocking collectives  43.3 us (12%)
  starting transfers between devices  26.5 us (8%)
  matrix products  10.8 us (3%)
  loops' own time  10.3 us (3%)
    unnamed x52, local copies, waits for them, and re-layouts  50.3 us
    psum x1, blocking collectives, on_device(): mixed_rows = lax.psum(partial_value, 'req').astype(jnp.bfloat16)  43.3 us
    dynamic_update_slice x16, local copies, waits for them, and re-layouts, on_device(): lax.scan(advance, (start_flat, start_flat), sliced)  31.3 us
    while x48, local copies, waits for them, and re-layouts  29.4 us
    all_to_all x1, waiting for transfers between devices, on_device(): lax.all_to_all(projected, 'req', split_axis=3, concat_axis=2, tiled=True)  23.9 us
    dynamic_slice x16, other arithmetic, on_device(): lax.scan(advance, (start_flat, start_flat), sliced)  20.9 us
    reduce_sum x16, other arithmetic, advance(): result = jnp.sum(spread(step_c) * current, axis=0)  14.9 us
    all_to_all x1, waiting for transfers between devices, on_device(): lax.all_to_all(chosen.reshape(state_size, all_reqs, channels), 'req', spl...  14.4 us
  transfers between devices with their start and end apart: 5, of which 3 were waited for; matrix products, arithmetic and copies ran while one was open for 16% of the time, Pallas kernels for 0%

profile of v1, /device:TPU:0, one launch (start us, length us, event | category | flops | bytes accessed | tf_op | source)
XLA Modules:
  0.0 348.0 jit_solution(10017953270379130450)
XLA Ops:
  0.6 3.9 %copy.80 = f32[8,3,2048]{0,1,2:T(4,128)} copy(bf16[8,3,2048]{2,0,1:T(8,128)(2,1)} %param.31) | data formatting | bytes 294912 | tf_op jit(solution)/shard_map/transpose | solution.py:49
  4.6 3.9 %bitcast_bitcast_fusion.1 = f32[2048,3,8]{2,1,0:T(4,128)} fusion(f32[8,3,2048]{0,1,2:T(4,128)} %copy.80), kind=kLoop, calls=%fused_computation.87 | loop fusion | bytes 393216
  8.5 5.2 %reshape.194 = f32[8,1,6144]{2,1,0:T(1,128)} reshape(f32[2048,3,8]{2,1,0:T(4,128)} %bitcast_bitcast_fusion.1) | data formatting | bytes 393216
  13.7 7.3 %all-to-all-start.1 = ((f32[8,1,6144]{2,1,0:T(1,128)}), f32[8,1,6144]{2,1,0:T(1,128)S(1)}, u32[]{:S(2)}, u32[]{:S(2)}) async-start(f32[8,1,6144]{2,1,0:T(1,128)} %reshape.194), calls=%async_computation.1 | async-start | bytes 393216 | tf_op jit(solution)/shard_map/all_to_all | solution.py:52
  26.2 4.8 %convolution_convert_fusion = bf16[128,4096]{1,0:T(8,128)(2,1)S(1)} fusion(bf16[1024,4096]{1,0:T(8,128)(2,1)} %param.21, f32[1024]{0:T(1024)S(1)} %copy-done.5, f32[128]{0:T(128)S(1)} %rsqrt.12, bf16[8,16,1024]{2,1,0:T(8,128)(2,1)S(1)} %copy-done.3), kind=kOutput, calls=%fused_computation.11 | convolution fusion | flops 1074790400 | bytes 9703936 | tf_op jit(solution)/shard_map/dot_general | solution.py:56
  31.2 8.8 %copy.83 = bf16[16,8,2,2048]{0,1,2,3:T(8,128)(2,1)} copy(bf16[16,8,2,2048]{3,1,2,0:T(8,128)(2,1)S(1)} %bitcast.194) | data formatting | bytes 2097152 | tf_op jit(solution)/shard_map/reshape | solution.py:57
  40.7 6.0 %all-to-all-start = ((f32[8,16,8,256]{3,1,2,0:T(8,128)}), f32[8,16,8,256]{3,1,2,0:T(8,128)S(1)}, u32[]{:S(2)}, u32[]{:S(2)}) async-start(f32[8,16,8,256]{3,1,2,0:T(8,128)} %fusion.27), calls=%async_computation | async-start | bytes 2097152 | tf_op jit(solution)/shard_map/all_to_all | solution.py:13
  46.7 7.5 %bitcast_bitcast_fusion = bf16[2048,2,8,16]{3,2,1,0:T(8,128)(2,1)} fusion(bf16[16,8,2,2048]{0,1,2,3:T(8,128)(2,1)} %copy.83), kind=kLoop, calls=%fused_computation.86 | loop fusion | bytes 2097152
  54.2 11.3 %reshape.192 = bf16[8,2,32768]{2,1,0:T(2,128)(2,1)} reshape(bf16[2048,2,8,16]{3,2,1,0:T(8,128)(2,1)} %bitcast_bitcast_fusion) | data formatting | bytes 2097152
  67.0 4.7 %reshape.195 = f32[2048,3,8]{2,1,0:T(4,128)} reshape(f32[8,6144]{1,0:T(8,128)S(1)} %reduce.2) | data formatting | bytes 393216
  71.7 3.5 copy.81
  76.2 6.0 %all-to-all-start.2 = ((bf16[8,2,32768]{2,1,0:T(2,128)(2,1)}), bf16[8,2,32768]{2,1,0:T(2,128)(2,1)S(1)}, u32[]{:S(2)}, u32[]{:S(2)}) async-start(bf16[8,2,32768]{2,1,0:T(2,128)(2,1)} %reshape.192), calls=%async_computation.2 | async-start | bytes 2097152 | tf_op jit(solution)/shard_map/all_to_all | solution.py:58
  83.1 23.9 %all-to-all-done.2 = bf16[8,2,32768]{2,1,0:T(2,128)(2,1)S(1)} async-done(((bf16[8,2,32768]{2,1,0:T(2,128)(2,1)}), bf16[8,2,32768]{2,1,0:T(2,128)(2,1)S(1)}, u32[]{:S(2)}, u32[]{:S(2)}) %all-to-all-start.2) | async-done | bytes 1048608 | tf_op jit(solution)/shard_map/all_to_all | solution.py:58
  107.0 7.5 %reshape.193 = bf16[2048,2,8,16]{3,2,1,0:T(8,128)(2,1)} reshape(bf16[8,2,32768]{2,1,0:T(2,128)(2,1)S(1)} %all-to-all-done.2) | data formatting | bytes 2097152
  114.6 8.9 %copy.84 = bf16[2,16,8,8,256]{4,2,3,1,0:T(8,128)(2,1)S(1)} copy(bf16[2,16,8,8,256]{1,2,0,4,3:T(8,128)(2,1)} %bitcast.181) | data formatting | bytes 2097152 | tf_op jit(solution)/shard_map/all_to_all | solution.py:58
  125.3 43.3 %all-reduce.1 = bf16[1024,160]{0,1:T(8,128)(2,1)} all-reduce(f32[1024,160]{0,1:T(8,128)S(1)} %fusion.37), channel_id=1, replica_groups=mesh['req'=8,'grp'=4] {'req'}, use_global_device_ids=true, to_apply=%region_1.2 | all-reduce | flops 163840 | bytes 983040 | tf_op jit(solution)/shard_map/psum | solution.py:75
  169.6 2.7 compare_select_fusion
  172.3 2.4 reshape.153
  176.0 129.5 %while.15 = (s32[]{:T(128)}, f32[16,16384]{1,0:T(8,128)S(1)}, f32[16,16384]{1,0:T(8,128)S(1)}, f32[16,16384]{1,0:T(8,128)}, f32[16,16384]{1,0:T(8,128)}, /*index...) while((s32[]{:T(128)}, f32[16,16384]{1,0:T(8,128)S(1)}, ...), condition=%wide.region_4.5_spmd.clone, body=%wide.region_2.4_spmd.clone.sunk | while | flops 1835075 | bytes 18522668 | solution.py:112
  182.1 2.0 dynamic_update_slice.6
  190.2 2.0 dynamic_update_slice.6
  198.3 2.0 dynamic_update_slice.6
  206.4 2.0 dynamic_update_slice.6
  214.6 2.0 dynamic_update_slice.6
  218.2 1.3 constant_dynamic-slice_fusion.6
  222.7 2.0 dynamic_update_slice.6
  226.3 1.3 constant_dynamic-slice_fusion.6
  230.8 2.0 dynamic_update_slice.6
  234.4 1.3 constant_dynamic-slice_fusion.6
  238.9 2.0 dynamic_update_slice.6
  242.5 1.3 constant_dynamic-slice_fusion.6
  247.0 1.9 dynamic_update_slice.6
  250.6 1.3 constant_dynamic-slice_fusion.6
  255.1 1.9 dynamic_update_slice.6
  263.1 1.9 dynamic_update_slice.6
  271.2 1.9 dynamic_update_slice.6
  279.3 1.9 dynamic_update_slice.6
  287.4 1.9 dynamic_update_slice.6
  295.4 1.9 dynamic_update_slice.6
  303.5 1.9 dynamic_update_slice.6
  305.5 1.5 copy.105
  307.0 1.5 fusion.16
  309.6 3.5 %all-to-all-start.3 = ((bf16[16,64,256]{2,0,1:T(8,128)(2,1)}), bf16[16,64,256]{2,0,1:T(8,128)(2,1)S(1)}, u32[]{:S(2)}, u32[]{:S(2)}) async-start(bf16[16,64,256]{2,0,1:T(8,128)(2,1)} %copy.88), calls=%async_computation.3 | async-start | bytes 1048576 | tf_op jit(solution)/shard_map/all_to_all | solution.py:117
  314.2 9.2 %all-to-all-done.3 = bf16[16,64,256]{2,0,1:T(8,128)(2,1)S(1)} async-done(((bf16[16,64,256]{2,0,1:T(8,128)(2,1)}), bf16[16,64,256]{2,0,1:T(8,128)(2,1)S(1)}, u32[]{:S(2)}, u32[]{:S(2)}) %all-to-all-start.3) | async-done | bytes 524320 | tf_op jit(solution)/shard_map/all_to_all | solution.py:117
  323.4 3.8 %all-to-all-start.4 = ((f32[16,64,256]{2,0,1:T(8,128)}), f32[16,64,256]{2,0,1:T(8,128)S(1)}, u32[]{:S(2)}, u32[]{:S(2)}) async-start(f32[16,64,256]{2,0,1:T(8,128)} %bitcast.147), calls=%async_computation.4 | async-start | bytes 2097152 | tf_op jit(solution)/shard_map/all_to_all | solution.py:124
  327.6 3.0 fusion.2
  331.5 14.4 %all-to-all-done.4 = f32[16,64,256]{2,0,1:T(8,128)S(1)} async-done(((f32[16,64,256]{2,0,1:T(8,128)}), f32[16,64,256]{2,0,1:T(8,128)S(1)}, u32[]{:S(2)}, u32[]{:S(2)}) %all-to-all-start.4) | async-done | bytes 1048608 | tf_op jit(solution)/shard_map/all_to_all | solution.py:124
  346.4 1.6 copy.93
  (302 shorter events, 99.0 us)
Async XLA Ops:
  0.6 124.3 %copy-start = (bf16[256,160]{0,1:T(8,128)(2,1)S(1)}, bf16[256,160]{0,1:T(8,128)(2,1)}, u32[]{:S(2)}) copy-start(bf16[256,160]{0,1:T(8,128)(2,1)} %param.24) | copy-start | bytes 245764
  8.5 12.5 %copy-start.13 = (s32[64]{0:T(128)S(1)}, s32[64]{0:T(128)}, u32[]{:S(2)}) copy-start(s32[64]{0:T(128)} %param.33) | copy-start | bytes 772
  8.5 12.5 %copy-start.4 = (f32[8,16,2048]{2,1,0:T(8,128)S(1)}, f32[8,16,2048]{2,1,0:T(8,128)}, u32[]{:S(2)}) copy-start(f32[8,16,2048]{2,1,0:T(8,128)} %param.30) | copy-start | bytes 3145732
  8.5 17.2 %copy-start.14 = (s32[64]{0:T(128)S(1)}, s32[64]{0:T(128)}, u32[]{:S(2)}) copy-start(s32[64]{0:T(128)} %param.32) | copy-start | bytes 772
  8.5 17.4 %copy-start.3 = (bf16[8,16,1024]{2,1,0:T(8,128)(2,1)S(1)}, bf16[8,16,1024]{2,1,0:T(8,128)(2,1)}, u32[]{:S(2)}) copy-start(bf16[8,16,1024]{2,1,0:T(8,128)(2,1)} %param.19) | copy-start | bytes 786436
  8.5 17.7 %copy-start.5 = (f32[1024]{0:T(1024)S(1)}, f32[1024]{0:T(1024)}, u32[]{:S(2)}) copy-start(f32[1024]{0:T(1024)} %param.20) | copy-start | bytes 12292
  13.7 27.0 %all-to-all-start.1 = ((f32[8,1,6144]{2,1,0:T(1,128)}), f32[8,1,6144]{2,1,0:T(1,128)S(1)}, u32[]{:S(2)}, u32[]{:S(2)}) async-start(f32[8,1,6144]{2,1,0:T(1,128)} %reshape.194), calls=%async_computation.1 | async-start | bytes 393216 | tf_op jit(solution)/shard_map/all_to_all | solution.py:52
  26.2 4.8 %copy-start.10 = (s32[64]{0:T(128)S(1)}, s32[64]{0:T(128)}, u32[]{:S(2)}) copy-start(s32[64]{0:T(128)} %param.35) | copy-start | bytes 772
  40.7 35.4 %all-to-all-start = ((f32[8,16,8,256]{3,1,2,0:T(8,128)}), f32[8,16,8,256]{3,1,2,0:T(8,128)S(1)}, u32[]{:S(2)}, u32[]{:S(2)}) async-start(f32[8,16,8,256]{3,1,2,0:T(8,128)} %fusion.27), calls=%async_computation | async-start | bytes 2097152 | tf_op jit(solution)/shard_map/all_to_all | solution.py:13
  54.2 11.3 %copy-start.7 = (f32[4,256]{1,0:T(4,128)S(1)}, f32[4,256]{1,0:T(4,128)}, u32[]{:S(2)}) copy-start(f32[4,256]{1,0:T(4,128)} %param.22) | copy-start | bytes 12292
  54.2 11.3 %copy-start.6 = (f32[16,256]{1,0:T(8,128)S(1)}, f32[16,256]{1,0:T(8,128)}, u32[]{:S(2)}) copy-start(f32[16,256]{1,0:T(8,128)} %param.27) | copy-start | bytes 49156
  76.2 30.9 %all-to-all-start.2 = ((bf16[8,2,32768]{2,1,0:T(2,128)(2,1)}), bf16[8,2,32768]{2,1,0:T(2,128)(2,1)S(1)}, u32[]{:S(2)}, u32[]{:S(2)}) async-start(bf16[8,2,32768]{2,1,0:T(2,128)(2,1)} %reshape.192), calls=%async_computation.2 | async-start | bytes 2097152 | tf_op jit(solution)/shard_map/all_to_all | solution.py:58
  114.6 9.9 %copy-start.8 = (f32[256]{0:T(256)S(1)}, f32[256]{0:T(256)}, u32[]{:S(2)}) copy-start(f32[256]{0:T(256)} %param.23) | copy-start | bytes 3076
  123.5 1.0 copy-start.2
  123.5 46.1 %copy-start.11 = (bf16[128,256]{1,0:T(8,128)(2,1)S(1)}, bf16[128,256]{1,0:T(8,128)(2,1)}, u32[]{:S(2)}) copy-start(bf16[128,256]{1,0:T(8,128)(2,1)} %param.25) | copy-start | bytes 196612
  123.5 46.1 %copy-start.12 = (f32[256]{0:T(256)S(1)}, f32[256]{0:T(256)}, u32[]{:S(2)}) copy-start(f32[256]{0:T(256)} %param.26) | copy-start | bytes 3076
  125.3 50.7 %copy-start.15 = (s32[64]{0:T(128)S(1)}, s32[64]{0:T(128)}, u32[]{:S(2)}) copy-start(s32[64]{0:T(128)} %param.34) | copy-start | bytes 772
  176.0 131.0 %copy-start.9 = (f32[256]{0:T(256)S(1)}, f32[256]{0:T(256)}, u32[]{:S(2)}) copy-start(f32[256]{0:T(256)} %param.28) | copy-start | bytes 3076
  309.6 13.8 %all-to-all-start.3 = ((bf16[16,64,256]{2,0,1:T(8,128)(2,1)}), bf16[16,64,256]{2,0,1:T(8,128)(2,1)S(1)}, u32[]{:S(2)}, u32[]{:S(2)}) async-start(bf16[16,64,256]{2,0,1:T(8,128)(2,1)} %copy.88), calls=%async_computation.3 | async-start | bytes 1048576 | tf_op jit(solution)/shard_map/all_to_all | solution.py:117
  323.4 22.4 %all-to-all-start.4 = ((f32[16,64,256]{2,0,1:T(8,128)}), f32[16,64,256]{2,0,1:T(8,128)S(1)}, u32[]{:S(2)}, u32[]{:S(2)}) async-start(f32[16,64,256]{2,0,1:T(8,128)} %bitcast.147), calls=%async_computation.4 | async-start | bytes 2097152 | tf_op jit(solution)/shard_map/all_to_all | solution.py:124
  327.6 20.4 %copy-start.1 = (bf16[256,160]{0,1:T(8,128)(2,1)S(1)}, bf16[256,160]{0,1:T(8,128)(2,1)}, u32[]{:S(2)}) copy-start(bf16[256,160]{0,1:T(8,128)(2,1)} %param.24) | copy-start | bytes 245764
